TPU v7x, 32 devices: a whole 2x2x4 slice. The times are simulated.
32 devices in a mesh: lon: 8 (over z, core), mem: 4 (over y, x).
Axes of the slice: x: 2, y: 2, z: 4, core: 2. Of those that a mesh axis runs over, the one named last changes fastest.
Arguments:
- members: float32 [32, 4, 192, 256], P('mem', None, 'lon'), may hold values from -6 to 6
- courant_lon: float32 [4, 192, 256], P(None, 'lon'), may hold values from -0.55 to 0.55
- courant_lat: float32 [4, 192, 256], P(None, 'lon'), may hold values from -0.4 to 0.4
- vert_modes: float32 [2, 4], replicated, may hold values from -1 to 1
- horiz_modes: float32 [4, 192, 256], P(None, 'lon'), may hold values from -1 to 1
- obs_index: int32 [16384], P('lon'), may hold values from 0 to 24575
- obs_count: int32 [8], P('lon'), may hold values from 1024 to 2048, as said below
- obs_value: float32 [16384], P('lon'), may hold values from -6 to 6
- obs_var: float32 [16384], P('lon'), may hold values from 2 to 48
Outputs:
- prior_trajectories: float32 [32, 4, 192, 256], P('mem', None, 'lon')
- analysis_mean: float32 [4, 192, 256], P(None, 'lon')
Inputs may be any that keep to these rules, and one draw needn't show every extreme that they name: `obs_index`: index of a cell within the band's own block: level, then longitude within the band, then latitude. Each band uses its first obs_count slots; some band uses all 2048.
All inputs are finite; a program needn't handle non-finite values.
Results may differ from a plain program's by a relative error of at most 0.0001.
Values sent between devices are 32-bit elements; how exact they have to be, the bound alone decides.
A program may use at most 128 MiB of HBM per device.

v0:
```python
import jax
import jax.numpy as jnp
from jax import lax
from jax.sharding import PartitionSpec as P

KV = 2
KH = 4
ADV_STEPS = 2


def padded(block, sides, width):
    for axis, dim in sides:
        count = lax.axis_size(axis)
        forward = [(i, i + 1) for i in range(count - 1)]
        forward.append((count - 1, 0))
        backward = [(target, source) for source, target in forward]
        low = lax.ppermute(
            lax.slice_in_dim(block, block.shape[dim] - width, None, axis=dim), axis, forward
        )
        high = lax.ppermute(lax.slice_in_dim(block, 0, width, axis=dim), axis, backward)
        block = jnp.concatenate([low, block, high], axis=dim)
    return block


def update(centre, western, eastern, flow_lon, flow_lat):
    zero_col = jnp.zeros_like(centre[..., :1])
    south_boundary = jnp.concatenate([zero_col, centre[..., :-1]], axis=-1)
    northern = jnp.concatenate([centre[..., 1:], zero_col], axis=-1)
    result = centre - jnp.maximum(flow_lon, 0.0) * (centre - western)
    result = result - jnp.minimum(flow_lon, 0.0) * (eastern - centre)
    result = result - jnp.maximum(flow_lat, 0.0) * (centre - south_boundary)
    result = result - jnp.minimum(flow_lat, 0.0) * (northern - centre)
    return result


def per_device(
    members,
    courant_lon,
    courant_lat,
    vert_modes,
    horiz_modes,
    obs_index,
    obs_count,
    obs_value,
    obs_var,
):
    mem_dev, layer_tally, band_width, lat_rows = members.shape
    sample_tally_overall = mem_dev * lax.axis_size("mem")
    rim_depth = ADV_STEPS
    stacked = jnp.concatenate(
        [members.reshape(mem_dev * layer_tally, band_width, lat_rows), courant_lon, courant_lat],
        axis=0,
    )
    extended = padded(stacked, (("lon", 1),), rim_depth)
    split_at = mem_dev * layer_tally
    prognostic_vector = extended[:split_at].reshape(
        mem_dev, layer_tally, band_width + 2 * rim_depth, lat_rows
    )
    flow_lon_ext = extended[split_at : split_at + layer_tally]
    meridional_wind_padded = extended[split_at + layer_tally :]
    for section in range(rim_depth):
        out_cols = band_width + 2 * (rim_depth - 1 - section)
        first_col = section + 1
        prognostic_vector = update(
            prognostic_vector[:, :, 1 : out_cols + 1],
            prognostic_vector[:, :, 0:out_cols],
            prognostic_vector[:, :, 2 : out_cols + 2],
            flow_lon_ext[:, first_col : first_col + out_cols],
            meridional_wind_padded[:, first_col : first_col + out_cols],
        )
    sample_centroid = lax.psum(jnp.sum(prognostic_vector, axis=0), "mem") / sample_tally_overall
    sample_departure = prognostic_vector - sample_centroid[None]
    norm_scale = (sample_tally_overall - 1) ** (-0.5)
    obs_slots = obs_index.shape[0]
    band_cells = band_width * lat_rows
    level_idx = obs_index // band_cells
    within = obs_index % band_cells
    anomaly_obs = jnp.take(sample_departure.reshape(mem_dev, -1), obs_index, axis=1)
    mean_obs = jnp.take(sample_centroid.reshape(-1), obs_index)
    vert_obs = jnp.take(vert_modes, level_idx, axis=1)
    horiz_obs = jnp.take(horiz_modes.reshape(KH, -1), within, axis=1)
    modes_obs = (vert_obs[:, None, :] * horiz_obs[None, :, :]).reshape(KV * KH, obs_slots)
    live_mask = (jnp.arange(obs_slots, dtype=jnp.int32) < obs_count[0]).astype(jnp.float32)
    obs_perts = (
        anomaly_obs[:, None, :] * modes_obs[None, :, :] * (live_mask * norm_scale)[None, None, :]
    )
    obs_perts = obs_perts.reshape(mem_dev * KV * KH, obs_slots)
    inv_var = live_mask / obs_var
    innovation = obs_value - mean_obs
    all_perts = lax.all_gather(obs_perts, "mem", axis=0, tiled=True)
    gram_part = jnp.dot(all_perts * inv_var[None, :], all_perts.T, precision=lax.Precision.HIGHEST)
    side_part = jnp.dot(all_perts, inv_var * innovation, precision=lax.Precision.HIGHEST)
    gram_matrix, right_side = lax.psum((gram_part, side_part), "lon")
    system = jnp.eye(gram_matrix.shape[0], dtype=jnp.float32) + gram_matrix
    factor = jnp.linalg.cholesky(system)
    weights = jax.scipy.linalg.cho_solve((factor, True), right_side)
    w_mat = weights.reshape(sample_tally_overall, KV * KH)
    w_local = lax.dynamic_slice_in_dim(w_mat, lax.axis_index("mem") * mem_dev, mem_dev, 0)
    mode_coef = jnp.einsum(
        "mk,mlij->klij", w_local, sample_departure, precision=lax.Precision.HIGHEST
    )
    mode_coef = mode_coef.reshape(KV, KH, layer_tally, band_width, lat_rows)
    inc_part = (
        jnp.einsum(
            "al,bij,ablij->lij", vert_modes, horiz_modes, mode_coef, precision=lax.Precision.HIGHEST
        )
        * norm_scale
    )
    posterior_adjustment = lax.psum(inc_part, "mem")
    return (prognostic_vector, sample_centroid + posterior_adjustment)


def solution(mesh):
    placed = (
        P("mem", None, "lon", None),
        P(None, "lon", None),
        P(None, "lon", None),
        P(),
        P(None, "lon", None),
        P("lon"),
        P("lon"),
        P("lon"),
        P("lon"),
    )
    return jax.shard_map(
        per_device,
        mesh=mesh,
        in_specs=placed,
        out_specs=(P("mem", None, "lon", None), P(None, "lon", None)),
        check_vma=False,
    )
```

profile of v0, /device:TPU:0, one launch (start us, length us, event | category | flops | bytes accessed | tf_op | source)
XLA Modules:
  0.0 332.7 jit_solution(16638624239704680310)
XLA Ops:
  7.2 1.2 pad_maximum_fusion.5
  8.4 0.5 collective-permute-start
  8.9 4.1 %collective-permute-start.1 = (f32[40,2,256]{2,1,0:T(2,128)S(1)}, f32[40,2,256]{2,1,0:T(2,128)S(1)}, u32[]{:S(2)}, u32[]{:S(2)}) collective-permute-start(f32[40,2,256]{2,1,0:T(2,128)S(1)} %get-tuple-element.36), channel_id=1, source_target_pairs={{4,0},{8,4},{12,8},{16,12},{20,16},{24,20},{28,24},{0,28},{5,1},{9... | collective-permute-start | bytes 245768 | tf_op jit(solution)/shard_map/ppermute | solution.py:20
  13.0 0.7 compare_and_fusion.1
  13.8 0.7 fusion.30
  14.5 0.8 copy.32
  15.2 5.5 %gather_fusion.1 = f32[2048,2]{1,0:T(8,128)S(1)} fusion(f32[2,4]{0,1:T(4,128)S(1)} %copy.32, s32[2048]{0:T(1024)S(1)} %get-tuple-element.46), kind=kCustom, calls=%fused_computation.1 | custom fusion | bytes 40960 | tf_op jit(solution)/shard_map/jit(_take)/gather | solution.py:80
  20.7 0.3 select_bitcast_fusion.1
  21.0 0.3 copy.33
  21.4 2.3 copy.34
  23.6 7.4 %gather_fusion.2 = f32[2048,4]{1,0:T(8,128)S(1)} fusion(f32[4,6144]{0,1:T(8,128)} %bitcast.119, s32[2048]{0:T(1024)S(1)} %get-tuple-element.47), kind=kCustom, calls=%fused_computation.2 | custom fusion | bytes 73728 | tf_op jit(solution)/shard_map/jit(_take)/gather | solution.py:81
  31.1 0.3 select_bitcast_fusion
  31.4 0.3 copy.35
  32.9 0.4 fusion.43
  33.4 0.7 fusion.9
  34.1 0.3 fusion.42
  34.4 1.2 fusion.39
  35.6 41.8 %all-reduce.9.cloned.1.call-done = f32[4,24,256]{2,1,0:T(8,128)} async-done(((f32[4,24,256]{2,1,0:T(8,128)}), f32[4,24,256]{2,1,0:T(8,128)}) %all-reduce.9.cloned.1.call-update) | async-done | bytes 98320 | tf_op jit(solution)/shard_map/psum | solution.py:71
  77.5 0.9 broadcast_multiply_fusion
  78.5 6.6 %copy.30 = f32[8,4,24,256]{0,3,2,1:T(8,128)} copy(f32[8,4,24,256]{3,2,1,0:T(8,128)S(1)} %broadcast_subtract_fusion) | data formatting | bytes 1572864 | tf_op jit(solution)/shard_map/sub | solution.py:72
  85.1 11.8 %gather_fusion.3 = f32[2048]{0:T(1024)S(1)} fusion(f32[24576]{0:T(1024)S(1)} %bitcast.112, s32[2048]{0:T(1024)S(1)} %get-tuple-element.45), kind=kCustom, calls=%fused_computation.3 | custom fusion | bytes 24576 | tf_op jit(solution)/shard_map/jit(_take)/gather | solution.py:79
  96.9 10.0 %gather_fusion = f32[2048,8]{1,0:T(8,128)S(1)} fusion(f32[8,24576]{0,1:T(8,128)} %bitcast.113, s32[2048]{0:T(1024)S(1)} %get-tuple-element.45), kind=kCustom, calls=%fused_computation | custom fusion | bytes 139264 | tf_op jit(solution)/shard_map/jit(_take)/gather | solution.py:78
  107.0 0.3 select_bitcast_fusion.2
  107.6 0.9 bitcast_multiply_fusion
  108.8 35.2 %all-gather.2.cloned.1.call-done = f32[256,2048]{1,0:T(8,128)} async-done(((f32[64,2048]{1,0:T(8,128)}), f32[256,2048]{1,0:T(8,128)}) %all-gather.2.cloned.1.call-update) | async-done | bytes 2097168 | tf_op jit(solution)/shard_map/all_gather | solution.py:90
  144.0 5.0 %fusion = f32[256,256]{0,1:T(8,128)} fusion(f32[256,2048]{1,0:T(8,128)} %all-gather.2.cloned.1.call-done, f32[2048]{0:T(1024)S(1)} %get-tuple-element.19), kind=kOutput, calls=%fused_computation.6 | convolution fusion | flops 1611137024 | bytes 2367488 | tf_op jit(solution)/shard_map/dot_general | solution.py:91
  149.1 1.7 fusion.44
  150.8 16.6 %psum.30 = f32[256]{0:T(256)S(1)} all-reduce(f32[256]{0:T(256)S(1)} %bitcast.124), channel_id=1, replica_groups=mesh['lon'=8,'mem'=4] {'lon'}, use_global_device_ids=true, to_apply=%region_7.8 | all-reduce | flops 256 | bytes 2048 | tf_op jit(solution)/shard_map/psum | solution.py:93
  167.4 36.7 %all-reduce.11.cloned.1.call-done = f32[256,256]{0,1:T(8,128)} async-done(((f32[256,256]{0,1:T(8,128)}), f32[256,256]{0,1:T(8,128)}) %all-reduce.11.cloned.1.call-update) | async-done | bytes 262160 | tf_op jit(solution)/shard_map/psum | solution.py:93
  204.1 1.0 convert_add_fusion
  205.2 1.0 fusion.19
  206.2 11.7 %cholesky.50 = f32[128,128]{1,0:T(8,128)S(1)} custom-call(f32[128,128]{1,0:T(8,128)S(1)} %cholesky.118), custom_call_target="Cholesky" | custom-call | tf_op jit(solution)/shard_map/jit(cholesky)/cholesky | solution.py:95
  218.0 0.7 compare_reduce_fusion.1
  218.7 9.8 %custom-call.18 = f32[1,128,128]{1,2,0:T(8,128)S(1)} custom-call(f32[1,128,128]{2,1,0:T(8,128)S(1)} %get-tuple-element.44), custom_call_target="InvertDiagBlocksLowerTriangular" | custom-call | tf_op jit(solution)/shard_map/jit(cholesky)/cholesky | solution.py:95
  229.0 11.7 %cholesky.105 = f32[128,128]{1,0:T(8,128)S(1)} custom-call(f32[128,128]{1,0:T(8,128)S(1)} %convolution_subtract_fusion), custom_call_target="Cholesky" | custom-call | tf_op jit(solution)/shard_map/jit(cholesky)/cholesky | solution.py:95
  240.7 0.6 compare_reduce_fusion
  242.6 3.8 %while.1 = (s32[]{:T(128)}, f32[256,256]{1,0:T(8,128)S(1)}, s32[2,2]{1,0:T(2,128)S(1)}, f32[2,128,128]{2,1,0:T(8,128)S(1)}, s32[]{:T(128)}) while((s32[]{:T(128)}, f32[256,256]{1,0:T(8,128)S(1)}, s32[2,2]{1,0:T(2,128)S(1)}, f32[2,128,128]{2,1,0:T(8,128)S(1)}, s32[]{:T(128)}) %tuple.44), condition=%wide.while_cond, body=%wide.while_body.sunk | while | flops 2 | bytes 131189 | solution.py:96
  242.6 0.6 fusion.57
  243.2 1.3 bitcast_dynamic-update-slice_fusion.2
  244.5 0.6 fusion.57
  245.2 1.3 bitcast_dynamic-update-slice_fusion.2
  246.4 19.9 %custom-call.19 = f32[2,128,128]{1,2,0:T(8,128)S(1)} custom-call(f32[2,128,128]{2,1,0:T(8,128)S(1)} %get-tuple-element.9), custom_call_target="InvertDiagBlocksLowerTriangular" | custom-call | tf_op jit(solution)/shard_map/jit(_cho_solve)/triangular_solve | solution.py:96
  267.6 13.6 %fusion.31 = f32[8,4,24,256]{3,0,2,1:T(8,128)S(1)} fusion(f32[8,4,24,256]{0,3,2,1:T(8,128)} %copy.30, f32[32,8]{1,0:T(8,128)S(1)} %reshape.169, s32[]{:T(128)S(6)} %select_n.71), kind=kOutput, calls=%fused_computation.98 | convolution fusion | flops 18874368 | bytes 1576964 | tf_op jit(solution)/shard_map/mk,mlij->klij/dot_general | solution.py:99
  281.5 0.6 multiply_reduce_fusion
  282.1 0.8 fusion.20
  283.0 0.7 bitcast_multiply_fusion.1
  283.6 41.0 %all-reduce.13.cloned.1.call-done = f32[4,24,256]{2,1,0:T(8,128)} async-done(((f32[4,24,256]{2,1,0:T(8,128)}), f32[4,24,256]{2,1,0:T(8,128)}) %all-reduce.13.cloned.1.call-update) | async-done | bytes 98320 | tf_op jit(solution)/shard_map/psum | solution.py:109
  324.6 1.5 fusion.38
  (69 shorter events, 3.6 us)
Async XLA Ops:
  7.2 70.3 %all-reduce.9.cloned.1.call-start = ((), (), s32[]{:S(2)}) async-start(), calls=%async_computation | async-start | bytes 196608 | tf_op jit(solution)/shard_map/psum | solution.py:71
  7.2 14.2 %copy-start.5 = (f32[4,24,256]{2,1,0:T(8,128)S(1)}, f32[4,24,256]{2,1,0:T(8,128)}, u32[]{:S(2)}) copy-start(f32[4,24,256]{2,1,0:T(8,128)} %param.13) | copy-start | bytes 294916
  8.4 24.1 %collective-permute-start = (f32[40,2,256]{2,1,0:T(2,128)S(1)}, f32[40,2,256]{2,1,0:T(2,128)S(1)}, u32[]{:S(2)}, u32[]{:S(2)}) collective-permute-start(f32[40,2,256]{2,1,0:T(2,128)S(1)} %get-tuple-element.35), channel_id=1, source_target_pairs={{0,4},{4,8},{8,12},{12,16},{16,20},{20,24},{24,28},{28,0},{1,5},{5... | collective-permute-start | bytes 245768 | tf_op jit(solution)/shard_map/ppermute | solution.py:17
  8.9 23.6 %collective-permute-start.1 = (f32[40,2,256]{2,1,0:T(2,128)S(1)}, f32[40,2,256]{2,1,0:T(2,128)S(1)}, u32[]{:S(2)}, u32[]{:S(2)}) collective-permute-start(f32[40,2,256]{2,1,0:T(2,128)S(1)} %get-tuple-element.36), channel_id=1, source_target_pairs={{4,0},{8,4},{12,8},{16,12},{20,16},{24,20},{28,24},{0,28},{5,1},{9... | collective-permute-start | bytes 245768 | tf_op jit(solution)/shard_map/ppermute | solution.py:20
  23.6 8.2 %copy-start.3 = (f32[4,24,256]{2,1,0:T(8,128)S(1)}, f32[4,24,256]{2,1,0:T(8,128)}, u32[]{:S(2)}) copy-start(f32[4,24,256]{2,1,0:T(8,128)} %param.11) | copy-start | bytes 294916
  23.6 8.2 %copy-start.4 = (f32[4,24,256]{2,1,0:T(8,128)S(1)}, f32[4,24,256]{2,1,0:T(8,128)}, u32[]{:S(2)}) copy-start(f32[4,24,256]{2,1,0:T(8,128)} %param.10) | copy-start | bytes 294916
  23.6 8.9 %copy-start.1 = (f32[8,4,24,256]{3,2,1,0:T(8,128)S(1)}, f32[8,4,24,256]{3,2,1,0:T(8,128)}, u32[]{:S(2)}) copy-start(f32[8,4,24,256]{3,2,1,0:T(8,128)} %param.9) | copy-start | bytes 2359300
  35.6 49.5 %copy-start.2 = (f32[8,4,24,256]{3,2,1,0:T(8,128)}, f32[8,4,24,256]{3,2,1,0:T(8,128)S(1)}, u32[]{:S(2)}) copy-start(f32[8,4,24,256]{3,2,1,0:T(8,128)S(1)} %get-tuple-element.22) | copy-start | bytes 2359300
  35.6 108.4 %all-gather.2.cloned.1.call-start = ((), (), s32[]{:S(2)}) async-start(), calls=%async_computation.1 | async-start | bytes 2621440 | tf_op jit(solution)/shard_map/all_gather | solution.py:90
  85.1 21.9 %copy-start.7 = (s32[2048]{0:T(1024)S(1)}, s32[2048]{0:T(1024)}, u32[]{:S(2)}) copy-start(s32[2048]{0:T(1024)} %param.14) | copy-start | bytes 24580
  85.1 21.9 %copy-start.8 = (f32[2048]{0:T(1024)S(1)}, f32[2048]{0:T(1024)}, u32[]{:S(2)}) copy-start(f32[2048]{0:T(1024)} %param.16) | copy-start | bytes 24580
  85.1 21.9 %copy-start.9 = (f32[2048]{0:T(1024)S(1)}, f32[2048]{0:T(1024)}, u32[]{:S(2)}) copy-start(f32[2048]{0:T(1024)} %param.17) | copy-start | bytes 24580
  107.0 1.6 copy-start.10
  108.5 95.6 %all-reduce.11.cloned.1.call-start = ((), (), s32[]{:S(2)}) async-start(), calls=%async_computation.2 | async-start | bytes 524288 | tf_op jit(solution)/shard_map/psum | solution.py:93
  144.0 5.1 %copy-start = (f32[256,2048]{1,0:T(8,128)S(1)}, f32[256,2048]{1,0:T(8,128)}, u32[]{:S(2)}) copy-start(f32[256,2048]{1,0:T(8,128)} %all-gather.2.cloned.1.call-done) | copy-start | bytes 6291460
  149.0 175.6 %all-reduce.13.cloned.1.call-start = ((), (), s32[]{:S(2)}) async-start(), calls=%async_computation.3 | async-start | bytes 196608 | tf_op jit(solution)/shard_map/psum | solution.py:109
  281.2 43.4 %copy-start.6 = (f32[4,24,256]{2,1,0:T(8,128)S(1)}, f32[4,24,256]{2,1,0:T(8,128)}, u32[]{:S(2)}) copy-start(f32[4,24,256]{2,1,0:T(8,128)} %all-reduce.9.cloned.1.call-done) | copy-start | bytes 294916
Sparse Core Ops, SparseCore 0:
  35.7 41.7 all-reduce.8
  108.7 35.2 all-gather.1
  149.1 54.9 all-reduce.10
  283.8 40.8 all-reduce.12
where the time goes:
time: 333 us
  waiting for transfers between devices  155 us (47%)
  other arithmetic  67 us (20%)
  local copies, waits for them, and re-layouts  50.6 us (15%)
  matrix products  22.8 us (7%)
  blocking collectives  16.6 us (5%)
  between operations  16 us (5%)
  starting transfers between devices  4.77 us (1%)
    psum x1, waiting for transfers between devices, per_device(): lax.psum(jnp.sum(prognostic_vector, axis=0), 'mem') / sample_tally_overall  41.8 us
    psum x1, waiting for transfers between devices, per_device(): posterior_adjustment = lax.psum(inc_part, 'mem')  41 us
    psum x1, waiting for transfers between devices, per_device(): gram_matrix, right_side = lax.psum((gram_part, side_part), 'lon')  36.7 us
    all_gather x1, waiting for transfers between devices, per_device(): all_perts = lax.all_gather(obs_perts, 'mem', axis=0, tiled=True)  35.2 us
    another operation x7, other arithmetic, per_device(): factor = jnp.linalg.cholesky(system)  34.6 us
    another operation x4, other arithmetic, per_device(): weights = jax.scipy.linalg.cho_solve((factor, True), right_side)  20 us
    psum x1, blocking collectives, per_device(): gram_matrix, right_side = lax.psum((gram_part, side_part), 'lon')  16.6 us
    dot_general x1, matrix products, per_device(): jnp.einsum('mk,mlij->klij', w_local, sample_departure, precision=lax.Prec...  13.6 us
  transfers between devices with their start and end apart: 6, of which 4 were waited for; matrix products, arithmetic and copies ran while one was open for 6% of the time, Pallas kernels for 0%

commit v1 on v0

--- a/solution.py
+++ b/solution.py
@@ -87,7 +87,12 @@
     obs_perts = obs_perts.reshape(mem_dev * KV * KH, obs_slots)
     inv_var = live_mask / obs_var
     innovation = obs_value - mean_obs
-    all_perts = lax.all_gather(obs_perts, "mem", axis=0, tiled=True)
+    ring = [obs_perts]
+    for hop in range(3):
+        ring.append(lax.ppermute(ring[-1], "mem", [(dev, (dev + 1) % 4) for dev in range(4)]))
+    all_perts = jnp.roll(
+        jnp.concatenate(ring[::-1], axis=0), (lax.axis_index("mem") + 1) * ring[0].shape[0], axis=0
+    )
     gram_part = jnp.dot(all_perts * inv_var[None, :], all_perts.T, precision=lax.Precision.HIGHEST)
     side_part = jnp.dot(all_perts, inv_var * innovation, precision=lax.Precision.HIGHEST)
     gram_matrix, right_side = lax.psum((gram_part, side_part), "lon")

time: 333 us -> 337 us (1.012)
    ppermute x0 -> x3, waiting for transfers between devices: none -> 37.6 us  [per_device(): lax.ppermute(ring[-1], 'mem', [(dev, (dev + 1) % 4) for dev in range(4)])]
    all_gather x1 -> x0, waiting for transfers between devices: 35.2 us -> none  [per_device(): all_perts = lax.all_gather(obs_perts, 'mem', axis=0, tiled=True)]
  transfers between devices with their start and end apart: 6 -> 8, of which waited for: 4 -> 6; matrix products, arithmetic and copies ran while one was open for 6% -> 7% of each run, Pallas kernels for 0% -> 0%
where the time goes in v1:
time: 337 us; the launch traced here: 336 us
  waiting for transfers between devices  158 us (47%)
  other arithmetic  66.3 us (20%)
  local copies, waits for them, and re-layouts  52.9 us (16%)
  matrix products  22.1 us (7%)
  between operations  16 us (5%)
  blocking collectives  13.9 us (4%)
  starting transfers between devices  6.77 us (2%)
    psum x1, waiting for transfers between devices, per_device(): lax.psum(jnp.sum(prognostic_vector, axis=0), 'mem') / sample_tally_overall  41.8 us
    psum x1, waiting for transfers between devices, per_device(): posterior_adjustment = lax.psum(inc_part, 'mem')  41 us
    psum x1, waiting for transfers between devices, per_device(): gram_matrix, right_side = lax.psum((gram_part, side_part), 'lon')  37.7 us
    ppermute x3, waiting for transfers between devices, per_device(): lax.ppermute(ring[-1], 'mem', [(dev, (dev + 1) % 4) for dev in range(4)])  37.6 us
    another operation x7, other arithmetic, per_device(): factor = jnp.linalg.cholesky(system)  34.6 us
    another operation x4, other arithmetic, per_device(): weights = jax.scipy.linalg.cho_solve((factor, True), right_side)  20 us
    psum x1, blocking collectives, per_device(): gram_matrix, right_side = lax.psum((gram_part, side_part), 'lon')  13.9 us
    dot_general x1, matrix products, per_device(): jnp.einsum('mk,mlij->klij', w_local, sample_departure, precision=lax.Prec...  13.6 us
  transfers between devices with their start and end apart: 8, of which 6 were waited for; matrix products, arithmetic and copies ran while one was open for 7% of the time, Pallas kernels for 0%

profile of v1, /device:TPU:0, one launch (start us, length us, event | category | flops | bytes accessed | tf_op | source)
XLA Modules:
  0.0 336.1 jit_solution(8426013771274765417)
XLA Ops:
  7.2 1.2 pad_maximum_fusion.5
  8.4 0.5 collective-permute-start
  8.9 4.1 %collective-permute-start.1 = (f32[40,2,256]{2,1,0:T(2,128)S(1)}, f32[40,2,256]{2,1,0:T(2,128)S(1)}, u32[]{:S(2)}, u32[]{:S(2)}) collective-permute-start(f32[40,2,256]{2,1,0:T(2,128)S(1)} %get-tuple-element.36), channel_id=1, source_target_pairs={{4,0},{8,4},{12,8},{16,12},{20,16},{24,20},{28,24},{0,28},{5,1},{9... | collective-permute-start | bytes 245768 | tf_op jit(solution)/shard_map/ppermute | solution.py:20
  13.0 0.7 fusion.35
  13.7 0.7 compare_and_fusion.1
  14.4 3.0 copy.34
  17.5 7.4 %gather_fusion.2 = f32[2048,4]{1,0:T(8,128)S(1)} fusion(f32[4,6144]{0,1:T(8,128)} %bitcast.121, s32[2048]{0:T(1024)S(1)} %get-tuple-element.47), kind=kCustom, calls=%fused_computation.2 | custom fusion | bytes 73728 | tf_op jit(solution)/shard_map/jit(_take)/gather | solution.py:81
  24.9 0.3 select_bitcast_fusion
  25.7 5.5 %gather_fusion.1 = f32[2048,2]{1,0:T(8,128)S(1)} fusion(f32[2,4]{0,1:T(4,128)S(1)} %copy.32, s32[2048]{0:T(1024)S(1)} %get-tuple-element.46), kind=kCustom, calls=%fused_computation.1 | custom fusion | bytes 40960 | tf_op jit(solution)/shard_map/jit(_take)/gather | solution.py:80
  31.2 0.3 select_bitcast_fusion.1
  32.9 0.4 fusion.50
  33.4 0.7 fusion.12
  34.5 1.2 fusion.46
  35.7 41.8 %all-reduce.9.cloned.1.call-done = f32[4,24,256]{2,1,0:T(8,128)} async-done(((f32[4,24,256]{2,1,0:T(8,128)}), f32[4,24,256]{2,1,0:T(8,128)}) %all-reduce.9.cloned.1.call-update) | async-done | bytes 98320 | tf_op jit(solution)/shard_map/psum | solution.py:71
  77.6 0.9 broadcast_multiply_fusion
  78.5 6.6 %copy.30 = f32[8,4,24,256]{0,3,2,1:T(8,128)} copy(f32[8,4,24,256]{3,2,1,0:T(8,128)S(1)} %broadcast_subtract_fusion) | data formatting | bytes 1572864 | tf_op jit(solution)/shard_map/sub | solution.py:72
  85.2 10.0 %gather_fusion = f32[2048,8]{1,0:T(8,128)S(1)} fusion(f32[8,24576]{0,1:T(8,128)} %bitcast.115, s32[2048]{0:T(1024)S(1)} %get-tuple-element.45), kind=kCustom, calls=%fused_computation | custom fusion | bytes 139264 | tf_op jit(solution)/shard_map/jit(_take)/gather | solution.py:78
  95.3 11.8 %gather_fusion.3 = f32[2048]{0:T(1024)S(1)} fusion(f32[24576]{0:T(1024)S(1)} %bitcast.114, s32[2048]{0:T(1024)S(1)} %get-tuple-element.45), kind=kCustom, calls=%fused_computation.3 | custom fusion | bytes 24576 | tf_op jit(solution)/shard_map/jit(_take)/gather | solution.py:79
  107.1 0.3 select_bitcast_fusion.2
  107.8 1.5 collective-permute-start.2
  109.3 12.7 %collective-permute-done.2 = f32[64,2048]{1,0:T(8,128)S(1)} collective-permute-done((f32[64,2048]{1,0:T(8,128)S(1)}, f32[64,2048]{1,0:T(8,128)S(1)}, u32[]{:S(2)}, u32[]{:S(2)}) %collective-permute-start.2) | collective-permute-done | bytes 524320 | tf_op jit(solution)/shard_map/ppermute | solution.py:92
  122.0 0.5 collective-permute-start.3
  122.5 12.7 %collective-permute-done.3 = f32[64,2048]{1,0:T(8,128)S(1)} collective-permute-done((f32[64,2048]{1,0:T(8,128)S(1)}, f32[64,2048]{1,0:T(8,128)S(1)}, u32[]{:S(2)}, u32[]{:S(2)}) %collective-permute-start.3) | collective-permute-done | bytes 524320 | tf_op jit(solution)/shard_map/ppermute | solution.py:92
  135.4 12.2 %collective-permute-done.4 = f32[64,2048]{1,0:T(8,128)S(1)} collective-permute-done((f32[64,2048]{1,0:T(8,128)S(1)}, f32[64,2048]{1,0:T(8,128)S(1)}, u32[]{:S(2)}, u32[]{:S(2)}) %collective-permute-start.4) | collective-permute-done | bytes 524320 | tf_op jit(solution)/shard_map/ppermute | solution.py:92
  148.0 1.9 copy-done
  149.9 2.7 fusion
  152.6 3.3 fusion.3
  155.9 13.9 %psum.30 = f32[256]{0:T(256)S(1)} all-reduce(f32[256]{0:T(256)S(1)} %bitcast.126), channel_id=1, replica_groups=mesh['lon'=8,'mem'=4] {'lon'}, use_global_device_ids=true, to_apply=%region_7.8 | all-reduce | flops 256 | bytes 2048 | tf_op jit(solution)/shard_map/psum | solution.py:98
  169.8 37.7 %all-reduce.11.cloned.1.call-done = f32[256,256]{0,1:T(8,128)} async-done(((f32[256,256]{0,1:T(8,128)}), f32[256,256]{0,1:T(8,128)}) %all-reduce.11.cloned.1.call-update) | async-done | bytes 262160 | tf_op jit(solution)/shard_map/psum | solution.py:98
  207.5 1.0 convert_add_fusion
  208.6 1.0 fusion.24
  209.6 11.7 %cholesky.50 = f32[128,128]{1,0:T(8,128)S(1)} custom-call(f32[128,128]{1,0:T(8,128)S(1)} %cholesky.118), custom_call_target="Cholesky" | custom-call | tf_op jit(solution)/shard_map/jit(cholesky)/cholesky | solution.py:100
  221.4 9.8 %custom-call.18 = f32[1,128,128]{1,2,0:T(8,128)S(1)} custom-call(f32[1,128,128]{2,1,0:T(8,128)S(1)} %get-tuple-element.44), custom_call_target="InvertDiagBlocksLowerTriangular" | custom-call | tf_op jit(solution)/shard_map/jit(cholesky)/cholesky | solution.py:100
  231.7 11.7 %cholesky.105 = f32[128,128]{1,0:T(8,128)S(1)} custom-call(f32[128,128]{1,0:T(8,128)S(1)} %convolution_subtract_fusion), custom_call_target="Cholesky" | custom-call | tf_op jit(solution)/shard_map/jit(cholesky)/cholesky | solution.py:100
  243.4 0.6 compare_reduce_fusion
  244.0 0.7 compare_reduce_fusion.1
  246.0 3.8 %while.1 = (s32[]{:T(128)}, f32[256,256]{1,0:T(8,128)S(1)}, s32[2,2]{1,0:T(2,128)S(1)}, f32[2,128,128]{2,1,0:T(8,128)S(1)}, s32[]{:T(128)}) while((s32[]{:T(128)}, f32[256,256]{1,0:T(8,128)S(1)}, s32[2,2]{1,0:T(2,128)S(1)}, f32[2,128,128]{2,1,0:T(8,128)S(1)}, s32[]{:T(128)}) %tuple.44), condition=%wide.while_cond, body=%wide.while_body.sunk | while | flops 2 | bytes 131181 | solution.py:101
  246.0 0.6 fusion.61
  246.6 1.3 bitcast_dynamic-update-slice_fusion.2
  247.9 0.6 fusion.61
  248.5 1.3 bitcast_dynamic-update-slice_fusion.2
  249.8 19.9 %custom-call.19 = f32[2,128,128]{1,2,0:T(8,128)S(1)} custom-call(f32[2,128,128]{2,1,0:T(8,128)S(1)} %get-tuple-element.9), custom_call_target="InvertDiagBlocksLowerTriangular" | custom-call | tf_op jit(solution)/shard_map/jit(_cho_solve)/triangular_solve | solution.py:101
  271.0 13.6 %fusion.36 = f32[8,4,24,256]{3,0,2,1:T(8,128)S(1)} fusion(f32[8,4,24,256]{0,3,2,1:T(8,128)} %copy.30, f32[32,8]{1,0:T(8,128)S(1)} %reshape.169, s32[]{:T(128)S(6)} %select_n.85), kind=kOutput, calls=%fused_computation.109 | convolution fusion | flops 18874368 | bytes 1576964 | tf_op jit(solution)/shard_map/mk,mlij->klij/dot_general | solution.py:104
  284.9 0.6 multiply_reduce_fusion
  285.5 0.8 fusion.25
  286.3 0.7 bitcast_multiply_fusion.1
  287.0 41.0 %all-reduce.13.cloned.1.call-done = f32[4,24,256]{2,1,0:T(8,128)} async-done(((f32[4,24,256]{2,1,0:T(8,128)}), f32[4,24,256]{2,1,0:T(8,128)}) %all-reduce.13.cloned.1.call-update) | async-done | bytes 98320 | tf_op jit(solution)/shard_map/psum | solution.py:114
  328.0 1.5 fusion.45
  (80 shorter events, 5.0 us)
Async XLA Ops:
  7.2 18.4 %copy-start.10 = (f32[2,4]{1,0:T(2,128)S(1)}, f32[2,4]{1,0:T(2,128)}, u32[]{:S(2)}) copy-start(f32[2,4]{1,0:T(2,128)} %param.12) | copy-start | bytes 100
  7.2 70.4 %all-reduce.9.cloned.1.call-start = ((), (), s32[]{:S(2)}) async-start(), calls=%async_computation | async-start | bytes 196608 | tf_op jit(solution)/shard_map/psum | solution.py:71
  8.4 24.2 %collective-permute-start = (f32[40,2,256]{2,1,0:T(2,128)S(1)}, f32[40,2,256]{2,1,0:T(2,128)S(1)}, u32[]{:S(2)}, u32[]{:S(2)}) collective-permute-start(f32[40,2,256]{2,1,0:T(2,128)S(1)} %get-tuple-element.35), channel_id=1, source_target_pairs={{0,4},{4,8},{8,12},{12,16},{16,20},{20,24},{24,28},{28,0},{1,5},{5... | collective-permute-start | bytes 245768 | tf_op jit(solution)/shard_map/ppermute | solution.py:17
  8.9 23.7 %collective-permute-start.1 = (f32[40,2,256]{2,1,0:T(2,128)S(1)}, f32[40,2,256]{2,1,0:T(2,128)S(1)}, u32[]{:S(2)}, u32[]{:S(2)}) collective-permute-start(f32[40,2,256]{2,1,0:T(2,128)S(1)} %get-tuple-element.36), channel_id=1, source_target_pairs={{4,0},{8,4},{12,8},{16,12},{20,16},{24,20},{28,24},{0,28},{5,1},{9... | collective-permute-start | bytes 245768 | tf_op jit(solution)/shard_map/ppermute | solution.py:20
  17.5 14.4 %copy-start.3 = (f32[4,24,256]{2,1,0:T(8,128)S(1)}, f32[4,24,256]{2,1,0:T(8,128)}, u32[]{:S(2)}) copy-start(f32[4,24,256]{2,1,0:T(8,128)} %param.11) | copy-start | bytes 294916
  17.5 14.4 %copy-start.4 = (f32[4,24,256]{2,1,0:T(8,128)S(1)}, f32[4,24,256]{2,1,0:T(8,128)}, u32[]{:S(2)}) copy-start(f32[4,24,256]{2,1,0:T(8,128)} %param.10) | copy-start | bytes 294916
  17.5 15.2 %copy-start.1 = (f32[8,4,24,256]{3,2,1,0:T(8,128)S(1)}, f32[8,4,24,256]{3,2,1,0:T(8,128)}, u32[]{:S(2)}) copy-start(f32[8,4,24,256]{3,2,1,0:T(8,128)} %param.9) | copy-start | bytes 2359300
  35.6 49.5 %copy-start.2 = (f32[8,4,24,256]{3,2,1,0:T(8,128)}, f32[8,4,24,256]{3,2,1,0:T(8,128)S(1)}, u32[]{:S(2)}) copy-start(f32[8,4,24,256]{3,2,1,0:T(8,128)S(1)} %get-tuple-element.22) | copy-start | bytes 2359300
  35.7 171.8 %all-reduce.11.cloned.1.call-start = ((), (), s32[]{:S(2)}) async-start(), calls=%async_computation.1 | async-start | bytes 524288 | tf_op jit(solution)/shard_map/psum | solution.py:98
  95.2 11.8 %copy-start.7 = (s32[2048]{0:T(1024)S(1)}, s32[2048]{0:T(1024)}, u32[]{:S(2)}) copy-start(s32[2048]{0:T(1024)} %param.14) | copy-start | bytes 24580
  95.2 11.8 %copy-start.8 = (f32[2048]{0:T(1024)S(1)}, f32[2048]{0:T(1024)}, u32[]{:S(2)}) copy-start(f32[2048]{0:T(1024)} %param.16) | copy-start | bytes 24580
  95.2 11.8 %copy-start.9 = (f32[2048]{0:T(1024)S(1)}, f32[2048]{0:T(1024)}, u32[]{:S(2)}) copy-start(f32[2048]{0:T(1024)} %param.17) | copy-start | bytes 24580
  95.2 40.0 %copy-start.5 = (f32[4,24,256]{2,1,0:T(8,128)S(1)}, f32[4,24,256]{2,1,0:T(8,128)}, u32[]{:S(2)}) copy-start(f32[4,24,256]{2,1,0:T(8,128)} %param.13) | copy-start | bytes 294916
  107.8 14.2 %collective-permute-start.2 = (f32[64,2048]{1,0:T(8,128)S(1)}, f32[64,2048]{1,0:T(8,128)S(1)}, u32[]{:S(2)}, u32[]{:S(2)}) collective-permute-start(f32[64,2048]{1,0:T(8,128)S(1)} %bitcast_multiply_fusion), channel_id=1, source_target_pairs={{0,1},{1,2},{2,3},{3,0},{4,5},{5,6},{6,7},{7,4},{8,9},{9,10},{10,1... | collective-permute-start | bytes 1572872 | tf_op jit(solution)/shard_map/ppermute | solution.py:92
  122.0 13.2 %collective-permute-start.3 = (f32[64,2048]{1,0:T(8,128)S(1)}, f32[64,2048]{1,0:T(8,128)S(1)}, u32[]{:S(2)}, u32[]{:S(2)}) collective-permute-start(f32[64,2048]{1,0:T(8,128)S(1)} %collective-permute-done.2), channel_id=1, source_target_pairs={{0,1},{1,2},{2,3},{3,0},{4,5},{5,6},{6,7},{7,4},{8,9},{9,10},{10,1... | collective-permute-start | bytes 1572872 | tf_op jit(solution)/shard_map/ppermute | solution.py:92
  135.3 12.3 %collective-permute-start.4 = (f32[64,2048]{1,0:T(8,128)S(1)}, f32[64,2048]{1,0:T(8,128)S(1)}, u32[]{:S(2)}, u32[]{:S(2)}) collective-permute-start(f32[64,2048]{1,0:T(8,128)S(1)} %collective-permute-done.3), channel_id=1, source_target_pairs={{0,1},{1,2},{2,3},{3,0},{4,5},{5,6},{6,7},{7,4},{8,9},{9,10},{10,1... | collective-permute-start | bytes 1572872 | tf_op jit(solution)/shard_map/ppermute | solution.py:92
  148.0 1.9 copy-start
  152.6 175.4 %all-reduce.13.cloned.1.call-start = ((), (), s32[]{:S(2)}) async-start(), calls=%async_computation.2 | async-start | bytes 196608 | tf_op jit(solution)/shard_map/psum | solution.py:114
  271.0 57.0 %copy-start.6 = (f32[4,24,256]{2,1,0:T(8,128)S(1)}, f32[4,24,256]{2,1,0:T(8,128)}, u32[]{:S(2)}) copy-start(f32[4,24,256]{2,1,0:T(8,128)} %all-reduce.9.cloned.1.call-done) | copy-start | bytes 294916
Sparse Core Ops, SparseCore 0:
  35.8 41.7 all-reduce.8
  152.7 54.7 all-reduce.10
  287.1 40.8 all-reduce.12
